TPU v7x, 128 devices: a whole 4x4x4 slice. The times are simulated.
128 devices in a mesh: dp: 8 (over z, core), label: 16 (over x, y).
Axes of the slice: x: 4, y: 4, z: 4, core: 2. Of those that a mesh axis runs over, the one named last changes fastest.
Arguments:
- features: bfloat16 [262144, 768], P(('dp', 'label')), may hold values from -6 to 6
- inst_ids: int32 [2048, 4], P(('dp', 'label')), may hold values from 0 to 15
- lab_ids: int32 [2048, 4], P(('dp', 'label')), may hold values from 0 to 15
- counts: int32 [2048], P(('dp', 'label')), may hold values from 0 to 4, as said below
- block_bits: int32 [2048, 4, 128, 128], P(('dp', 'label')), may hold values 0 or 1
- centroids: bfloat16 [2048, 768], P('label'), may hold values from -40 to 40
Outputs:
- label_embed: bfloat16 [32768, 768], P(('dp', 'label'))
- membership: bfloat16 [32768, 2048], P(('dp', 'label'))
- targets: bfloat16 [262144, 768], P(('dp', 'label'))
Inputs may be any that keep to these rules, and one draw needn't show every extreme that they name: `lab_ids`: label block within the slot's label column. `counts`: in every draw one label column has all 4 slots used on every device.
All inputs are finite; a program needn't handle non-finite values. No bound on the sum of `block_bits` on one device may be relied on, other than what follows from the above.
Results may differ from a plain program's by a relative error of at most 0.008.
The roundings to bfloat16 on the way count: a program that leaves them out, or rounds other values in their place, can miss the bound.
Values may be sent and summed in bfloat16 or wider, within the bound.
No kernel may reach another device: no remote copies, remote signals or barrier semaphores. Data moves between devices by JAX's collectives and lax.ppermute only.
A program may use at most 128 MiB of HBM per device.

v0:
```python
import jax
import jax.numpy as jnp
from jax import lax
from jax.sharding import PartitionSpec as P

LB_DEV = 2
epsilon = 1e-05


def label_side(column_sums, centroids):
    embed32 = column_sums * lax.rsqrt(
        jnp.mean(column_sums * column_sums, axis=1, keepdims=True) + epsilon
    )
    label_embed = embed32.astype(jnp.bfloat16)
    all_rows = lax.all_gather(centroids, "label", axis=0, tiled=True)
    scores = jnp.einsum("rd,kd->rk", label_embed, all_rows, preferred_element_type=jnp.float32)
    row_peak = jnp.max(scores, axis=1, keepdims=True)
    lifted = jnp.exp(scores - row_peak)
    membership = (lifted / jnp.sum(lifted, axis=1, keepdims=True)).astype(jnp.bfloat16)
    mixed_rows = jnp.dot(membership, all_rows, preferred_element_type=jnp.float32)
    return (label_embed, membership, mixed_rows.astype(jnp.bfloat16))


def body(features, inst_ids, lab_ids, counts, block_bits, centroids):
    dest_count, slot_cap = inst_ids.shape
    block_size = block_bits.shape[-1]
    feat_width = features.shape[1]
    inst_blocks = features.reshape(-1, block_size, feat_width)
    gathered = inst_blocks[inst_ids]
    incidence = block_bits.astype(jnp.bfloat16)
    partials = jnp.einsum(
        "ncab,ncad->ncbd", incidence, gathered, preferred_element_type=jnp.float32
    ).astype(jnp.bfloat16)
    filled = jnp.arange(slot_cap)[None, :] < counts[:, None]
    tagged_ids = jnp.where(filled, lab_ids, -1)
    arrived, arrived_ids = (
        lax.all_to_all(partials, "label", split_axis=0, concat_axis=0, tiled=True),
        lax.all_to_all(tagged_ids, "label", split_axis=0, concat_axis=0, tiled=True),
    )
    share_rows = LB_DEV * block_size
    col_blocks = lax.axis_size("dp") * LB_DEV
    slot_total = dest_count * slot_cap
    flat_ids = arrived_ids.reshape(slot_total)
    selector = (flat_ids[None, :] == jnp.arange(col_blocks)[:, None]).astype(jnp.bfloat16)
    column_sums = jnp.dot(
        selector,
        arrived.reshape(slot_total, block_size * feat_width),
        preferred_element_type=jnp.float32,
    )
    column_total = lax.psum(column_sums, "dp")
    embed_all, member_all, column_mixed = label_side(
        column_total.reshape(col_blocks * block_size, feat_width), centroids
    )
    offset = lax.axis_index("dp") * share_rows
    label_embed = lax.dynamic_slice_in_dim(embed_all, offset, share_rows, 0)
    membership = lax.dynamic_slice_in_dim(member_all, offset, share_rows, 0)
    mixed_blocks = column_mixed.reshape(col_blocks, block_size, feat_width)
    picked = mixed_blocks[jnp.maximum(arrived_ids, 0)]
    picked = jnp.where((arrived_ids >= 0)[:, :, None, None], picked, jnp.zeros_like(picked))
    returned = lax.all_to_all(picked, "label", split_axis=0, concat_axis=0, tiled=True)
    contrib = jnp.einsum("ncab,ncbd->ncad", incidence, returned, preferred_element_type=jnp.float32)
    owner_map = (
        inst_ids.reshape(slot_total)[None, :] == jnp.arange(inst_blocks.shape[0])[:, None]
    ).astype(jnp.float32)
    raw_targets = jnp.dot(
        owner_map,
        contrib.reshape(slot_total, block_size * feat_width),
        precision=lax.Precision.HIGHEST,
    )
    raw_targets = raw_targets.reshape(-1, feat_width)
    targets = raw_targets * lax.rsqrt(
        jnp.mean(raw_targets * raw_targets, axis=1, keepdims=True) + epsilon
    )
    return (label_embed, membership, targets.astype(jnp.bfloat16))


def solution(mesh):
    in_specs = (
        P(("dp", "label"), None),
        P(("dp", "label"), None),
        P(("dp", "label"), None),
        P(("dp", "label")),
        P(("dp", "label"), None, None, None),
        P("label", None),
    )
    out_specs = (P(("dp", "label"), None), P(("dp", "label"), None), P(("dp", "label"), None))
    return jax.shard_map(body, mesh=mesh, in_specs=in_specs, out_specs=out_specs, check_vma=False)
```

profile of v0, /device:TPU:61, one launch (start us, length us, event | category | flops | bytes accessed | tf_op | source)
XLA Modules:
  0.0 778.2 jit_solution(7269517425034337055)
XLA Ops:
  9.5 6.6 all-to-all-start
  17.0 7.3 gather_fusion
  24.3 10.8 %convert_bitcast_fusion = bf16[16,4,128,768]{2,3,1,0:T(8,128)(2,1)} fusion(bf16[16,4,128,768]{3,2,1,0:T(8,128)(2,1)} %bitcast.31, s32[16,4,128,128]{3,2,1,0:T(8,128)} %param.10), kind=kOutput, calls=%fused_computation.5 | convolution fusion | flops 1617952768 | bytes 29360128 | tf_op jit(solution)/shard_map/ncab,ncad->ncbd/dot_general | solution.py:31
  35.1 6.7 all-to-all-start.1
  43.1 219.6 %all-to-all-done.1 = bf16[16,4,128,768]{2,3,1,0:T(8,128)(2,1)} async-done(((bf16[16,4,128,768]{2,3,1,0:T(8,128)(2,1)}), bf16[16,4,128,768]{2,3,1,0:T(8,128)(2,1)}, u32[]{:S(2)}, u32[]{:S(2)}) %all-to-all-start.1) | async-done | bytes 12582944 | tf_op jit(solution)/shard_map/all_to_all | solution.py:37
  262.7 16.7 %copy.37 = bf16[8,8,128,768]{3,1,2,0:T(8,128)(2,1)} copy(bf16[8,8,128,768]{2,3,1,0:T(8,128)(2,1)} %bitcast.18) | data formatting | bytes 25165824
  279.4 9.0 %fusion.3 = f32[16,98304]{1,0:T(8,128)} fusion(bf16[64,98304]{1,0:T(8,128)(2,1)} %bitcast.34, s32[64]{0:T(128)S(1)} %eq.30), kind=kOutput, calls=%fused_computation.20 | convolution fusion | flops 201327616 | bytes 18874624 | tf_op jit(solution)/shard_map/dot_general | solution.py:45
  288.4 5.0 reshape.69
  294.3 91.9 %all-reduce.2.cloned.1.call-done = f32[2048,768]{1,0:T(8,128)} async-done(((f32[2048,768]{1,0:T(8,128)}), f32[2048,768]{1,0:T(8,128)}) %all-reduce.2.cloned.1.call-update) | async-done | bytes 6291472 | tf_op jit(solution)/shard_map/psum | solution.py:50
  386.2 3.4 multiply_reduce_fusion.1
  391.2 13.1 %fusion.7 = (f32[2048]{0:T(1024)S(1)}, f32[2048,2048]{0,1:T(8,128)}) fusion(bf16[2048,768]{1,0:T(8,128)(2,1)S(1)} %multiply_convert_fusion.1, bf16[2048,768]{1,0:T(8,128)(2,1)} %all-gather.2.cloned.1.call-done), kind=kOutput, calls=%fused_computation.32 | convolution fusion | flops 6446643200 | bytes 23076864 | tf_op jit(solution)/shard_map/rd,kd->rk/dot_general | solution.py:16
  404.4 8.1 %fusion = f32[2048]{0:T(1024)S(1)} fusion(f32[2048,2048]{0,1:T(8,128)} %get-tuple-element.15, f32[2048]{0:T(1024)S(1)} %get-tuple-element.14), kind=kLoop, calls=%fused_computation.4 | loop fusion | flops 8386560 | bytes 16793600 | tf_op jit(solution)/shard_map/reduce_sum | solution.py:19
  412.4 7.5 divide_convert_fusion
  419.9 7.3 convolution_convert_fusion
  427.3 7.1 gather_fusion.1
  434.4 16.6 %copy.34 = bf16[64,128,768]{1,2,0:T(8,128)(2,1)} copy(bf16[64,128,768]{2,1,0:T(8,128)(2,1)} %gather_fusion.1) | data formatting | bytes 25165824 | tf_op jit(solution)/shard_map/gather | solution.py:58
  451.0 10.6 %broadcast_select_fusion = bf16[16,4,128,768]{2,3,1,0:T(8,128)(2,1)} fusion(bf16[16,4,128,768]{2,3,1,0:T(8,128)(2,1)} %bitcast.32, pred[16,4]{1,0:T(8,128)(4,1)S(1)} %copy.33), kind=kLoop, calls=%fused_computation.6 | loop fusion | flops 6291456 | bytes 25165888 | tf_op jit(solution)/shard_map/jit(_where)/select_n | solution.py:59
  461.7 6.9 all-to-all-start.2
  473.2 232.2 %all-to-all-done.2 = bf16[16,4,128,768]{2,3,1,0:T(8,128)(2,1)} async-done(((bf16[16,4,128,768]{2,3,1,0:T(8,128)(2,1)}), bf16[16,4,128,768]{2,3,1,0:T(8,128)(2,1)}, u32[]{:S(2)}, u32[]{:S(2)}) %all-to-all-start.2) | async-done | bytes 12582944 | tf_op jit(solution)/shard_map/all_to_all | solution.py:60
  705.4 14.1 %convolution_bitcast_fusion = f32[16,4,128,768]{2,3,1,0:T(8,128)} fusion(bf16[16,4,128,768]{2,3,1,0:T(8,128)(2,1)} %all-to-all-done.2, s32[16,4,128,128]{3,2,1,0:T(8,128)} %param.10), kind=kOutput, calls=%fused_computation.7 | convolution fusion | flops 1611661312 | bytes 41943040 | tf_op jit(solution)/shard_map/ncab,ncbd->ncad/dot_general | solution.py:61
  719.5 25.1 %copy.38 = f32[8,8,128,768]{3,1,2,0:T(8,128)} copy(f32[8,8,128,768]{2,3,1,0:T(8,128)} %bitcast.29) | data formatting | bytes 50331648
  744.6 14.3 %fusion.4 = f32[16,98304]{1,0:T(8,128)} fusion(f32[64,98304]{1,0:T(8,128)} %bitcast.30, s32[64]{0:T(128)S(1)} %eq.34), kind=kOutput, calls=%fused_computation.21 | convolution fusion | flops 1207960576 | bytes 31457536 | tf_op jit(solution)/shard_map/dot_general | solution.py:65
  758.9 5.2 reshape.72
  764.1 3.4 multiply_reduce_fusion
  (45 shorter events, 14.1 us)
Async XLA Ops:
  8.0 9.0 %copy-start = (bf16[2048,768]{1,0:T(8,128)(2,1)S(1)}, bf16[2048,768]{1,0:T(8,128)(2,1)}, u32[]{:S(2)}) copy-start(bf16[2048,768]{1,0:T(8,128)(2,1)} %param.6) | copy-start | bytes 9437188
  9.5 25.5 %all-to-all-start = ((s32[16,1,4]{2,1,0:T(1,128)}), s32[16,1,4]{2,1,0:T(1,128)S(1)}, u32[]{:S(2)}, u32[]{:S(2)}) async-start(s32[16,1,4]{2,1,0:T(1,128)} %copy.27), calls=%async_computation | async-start | bytes 16384 | tf_op jit(solution)/shard_map/all_to_all | solution.py:38
  35.1 227.6 %all-to-all-start.1 = ((bf16[16,4,128,768]{2,3,1,0:T(8,128)(2,1)}), bf16[16,4,128,768]{2,3,1,0:T(8,128)(2,1)}, u32[]{:S(2)}, u32[]{:S(2)}) async-start(bf16[16,4,128,768]{2,3,1,0:T(8,128)(2,1)} %convert_bitcast_fusion), calls=%async_computation.1 | async-start | bytes 25165824 | tf_op jit(solution)/shard_map/all_to_all | solution.py:37
  41.7 344.4 %all-reduce.2.cloned.1.call-start = ((), (), s32[]{:S(2)}) async-start(), calls=%async_computation.3 | async-start | bytes 12582912 | tf_op jit(solution)/shard_map/psum | solution.py:50
  293.4 97.8 %all-gather.2.cloned.1.call-start = ((), (), s32[]{:S(2)}) async-start(), calls=%async_computation.4 | async-start | bytes 3342336 | tf_op jit(solution)/shard_map/all_gather | solution.py:15
  386.2 4.6 copy-start.3
  391.2 13.2 %copy-start.5 = (bf16[2048,768]{1,0:T(8,128)(2,1)}, bf16[2048,768]{1,0:T(8,128)(2,1)S(1)}, u32[]{:S(2)}) copy-start(bf16[2048,768]{1,0:T(8,128)(2,1)S(1)} %multiply_convert_fusion.1) | copy-start | bytes 9437188
  412.4 7.5 copy-start.7
  419.9 7.3 copy-start.4
  461.7 6.9 copy-start.6
  461.7 243.7 %all-to-all-start.2 = ((bf16[16,4,128,768]{2,3,1,0:T(8,128)(2,1)}), bf16[16,4,128,768]{2,3,1,0:T(8,128)(2,1)}, u32[]{:S(2)}, u32[]{:S(2)}) async-start(bf16[16,4,128,768]{2,3,1,0:T(8,128)(2,1)} %broadcast_select_fusion), calls=%async_computation.2 | async-start | bytes 25165824 | tf_op jit(solution)/shard_map/all_to_all | solution.py:60
  758.9 11.8 %copy-start.1 = (bf16[2048,768]{1,0:T(8,128)(2,1)S(1)}, bf16[2048,768]{1,0:T(8,128)(2,1)}, u32[]{:S(2)}) copy-start(bf16[2048,768]{1,0:T(8,128)(2,1)} %param.6) | copy-start | bytes 9437188
  764.1 4.6 copy-start.2
Sparse Core Ops, SparseCore 0:
  293.5 92.5 all-reduce.1
Sparse Core Ops, SparseCore 1:
  296.1 53.1 all-gather.1
where the time goes:
time: 780 us; the launch traced here: 778 us
  waiting for transfers between devices  544 us (70%)
  local copies, waits for them, and re-layouts  91.8 us (12%)
  matrix products  68.7 us (9%)
  other arithmetic  37.7 us (5%)
  starting transfers between devices  20.2 us (3%)
  between operations  15.6 us (2%)
    all_to_all x1, waiting for transfers between devices, body(): lax.all_to_all(picked, 'label', split_axis=0, concat_axis=0, tiled=True)  232 us
    all_to_all x1, waiting for transfers between devices, body(): lax.all_to_all(partials, 'label', split_axis=0, concat_axis=0, tiled=True)  220 us
    psum x1, waiting for transfers between devices, body(): column_total = lax.psum(column_sums, 'dp')  91.9 us
    unnamed x20, local copies, waits for them, and re-layouts  45.7 us
    gather x2, local copies, waits for them, and re-layouts, body(): picked = mixed_blocks[jnp.maximum(arrived_ids, 0)]  23.8 us
  transfers between devices with their start and end apart: 5, of which 3 were waited for; matrix products, arithmetic and copies ran while one was open for 4% of the time, Pallas kernels for 0%

commit v1 on v0

--- a/solution.py
+++ b/solution.py
@@ -47,7 +47,8 @@
         arrived.reshape(slot_total, block_size * feat_width),
         preferred_element_type=jnp.float32,
     )
-    column_total = lax.psum(column_sums, "dp")
+    terms = lax.all_gather(column_sums, "dp")
+    column_total = jnp.sum(terms, axis=0)
     embed_all, member_all, column_mixed = label_side(
         column_total.reshape(col_blocks * block_size, feat_width), centroids
     )

time: 780 us -> 950 us (1.22)
  waiting for transfers between devices: 544 us -> 687 us
  other arithmetic: 37.7 us -> 57.9 us
    all_gather x0 -> x1, waiting for transfers between devices: none -> 234 us  [body(): terms = lax.all_gather(column_sums, 'dp')]
    psum x1 -> x0, waiting for transfers between devices: 91.9 us -> none  [body(): column_total = lax.psum(column_sums, 'dp')]
    reduce_sum x0 -> x1, other arithmetic: none -> 20.2 us  [body(): column_total = jnp.sum(terms, axis=0)]
    all_gather x1, waiting for transfers between devices: 0.03 us -> 17.4 us  [label_side(): all_rows = lax.all_gather(centroids, 'label', axis=0, tiled=True)]
    all_to_all x1, waiting for transfers between devices: 232 us -> 215 us  [body(): lax.all_to_all(picked, 'label', split_axis=0, concat_axis=0, tiled=True)]
  transfers between devices with their start and end apart: 5 -> 5, of which waited for: 3 -> 4; matrix products, arithmetic and copies ran while one was open for 4% -> 6% of each run, Pallas kernels for 0% -> 0%
where the time goes in v1:
time: 950 us; the launch traced here: 939 us
  waiting for transfers between devices  687 us (72%)
  local copies, waits for them, and re-layouts  92 us (10%)
  matrix products  67.4 us (7%)
  other arithmetic  57.9 us (6%)
  starting transfers between devices  20.9 us (2%)
  between operations  14.2 us (1%)
    all_gather x1, waiting for transfers between devices, body(): terms = lax.all_gather(column_sums, 'dp')  234 us
    all_to_all x1, waiting for transfers between devices, body(): lax.all_to_all(partials, 'label', split_axis=0, concat_axis=0, tiled=True)  220 us
    all_to_all x1, waiting for transfers between devices, body(): lax.all_to_all(picked, 'label', split_axis=0, concat_axis=0, tiled=True)  215 us
    unnamed x20, local copies, waits for them, and re-layouts  45.7 us
    gather x2, local copies, waits for them, and re-layouts, body(): picked = mixed_blocks[jnp.maximum(arrived_ids, 0)]  24 us
    reduce_sum x1, other arithmetic, body(): column_total = jnp.sum(terms, axis=0)  20.2 us
  transfers between devices with their start and end apart: 5, of which 4 were waited for; matrix products, arithmetic and copies ran while one was open for 6% of the time, Pallas kernels for 0%

profile of v1, /device:TPU:61, one launch (start us, length us, event | category | flops | bytes accessed | tf_op | source)
XLA Modules:
  0.0 939.1 jit_solution(260971121001942598)
XLA Ops:
  8.7 6.6 all-to-all-start
  16.1 7.3 gather_fusion
  23.4 10.7 %convert_bitcast_fusion = bf16[16,4,128,768]{2,3,1,0:T(8,128)(2,1)} fusion(bf16[16,4,128,768]{3,2,1,0:T(8,128)(2,1)} %bitcast.32, s32[16,4,128,128]{3,2,1,0:T(8,128)} %param.10), kind=kOutput, calls=%fused_computation.5 | convolution fusion | flops 1617952768 | bytes 29360128 | tf_op jit(solution)/shard_map/ncab,ncad->ncbd/dot_general | solution.py:31
  34.1 6.7 all-to-all-start.1
  42.1 219.5 %all-to-all-done.1 = bf16[16,4,128,768]{2,3,1,0:T(8,128)(2,1)} async-done(((bf16[16,4,128,768]{2,3,1,0:T(8,128)(2,1)}), bf16[16,4,128,768]{2,3,1,0:T(8,128)(2,1)}, u32[]{:S(2)}, u32[]{:S(2)}) %all-to-all-start.1) | async-done | bytes 12582944 | tf_op jit(solution)/shard_map/all_to_all | solution.py:37
  261.7 16.7 %copy.37 = bf16[8,8,128,768]{3,1,2,0:T(8,128)(2,1)} copy(bf16[8,8,128,768]{2,3,1,0:T(8,128)(2,1)} %bitcast.19) | data formatting | bytes 25165824
  278.4 8.9 fusion.3
  288.4 234.1 %all-gather.6.cloned.1.call-done = f32[128,98304]{1,0:T(8,128)} async-done(((f32[16,98304]{1,0:T(8,128)}), f32[128,98304]{1,0:T(8,128)}) %all-gather.6.cloned.1.call-update) | async-done | bytes 50331664 | tf_op jit(solution)/shard_map/all_gather | solution.py:50
  522.4 20.2 %reduce_sum.36 = f32[16,98304]{1,0:T(8,128)} reduce(f32[8,16,98304]{2,1,0:T(8,128)} %bitcast.35, f32[]{:T(128)} %constant.7.clone.1), dimensions={0}, to_apply=%region_0.1 | reduce | flops 11010048 | bytes 56623108 | tf_op jit(solution)/shard_map/reduce_sum | solution.py:51
  542.6 5.0 reshape.69
  552.6 17.4 %all-gather.4.cloned.1.call-done = bf16[2048,768]{1,0:T(8,128)(2,1)} async-done(((bf16[128,768]{1,0:T(8,128)(2,1)}), bf16[2048,768]{1,0:T(8,128)(2,1)}) %all-gather.4.cloned.1.call-update) | async-done | bytes 3145744 | tf_op jit(solution)/shard_map/all_gather | solution.py:15
  570.0 12.0 %fusion.7 = (f32[2048]{0:T(1024)S(1)}, f32[2048,2048]{0,1:T(8,128)}) fusion(bf16[2048,768]{1,0:T(8,128)(2,1)S(1)} %multiply_convert_fusion.1, bf16[2048,768]{1,0:T(8,128)(2,1)} %all-gather.4.cloned.1.call-done), kind=kOutput, calls=%fused_computation.32 | convolution fusion | flops 6446643200 | bytes 23076864 | tf_op jit(solution)/shard_map/rd,kd->rk/dot_general | solution.py:16
  582.1 8.1 fusion
  590.2 7.5 divide_convert_fusion
  597.7 7.3 convolution_convert_fusion
  605.0 7.3 gather_fusion.1
  612.3 16.6 %copy.34 = bf16[64,128,768]{1,2,0:T(8,128)(2,1)} copy(bf16[64,128,768]{2,1,0:T(8,128)(2,1)} %gather_fusion.1) | data formatting | bytes 25165824 | tf_op jit(solution)/shard_map/gather | solution.py:59
  629.0 10.6 %broadcast_select_fusion = bf16[16,4,128,768]{2,3,1,0:T(8,128)(2,1)} fusion(bf16[16,4,128,768]{2,3,1,0:T(8,128)(2,1)} %bitcast.33, pred[16,4]{1,0:T(8,128)(4,1)S(1)} %copy.33), kind=kLoop, calls=%fused_computation.6 | loop fusion | flops 6291456 | bytes 25165888 | tf_op jit(solution)/shard_map/jit(_where)/select_n | solution.py:60
  639.6 7.4 all-to-all-start.2
  651.7 215.2 %all-to-all-done.2 = bf16[16,4,128,768]{2,3,1,0:T(8,128)(2,1)} async-done(((bf16[16,4,128,768]{2,3,1,0:T(8,128)(2,1)}), bf16[16,4,128,768]{2,3,1,0:T(8,128)(2,1)}, u32[]{:S(2)}, u32[]{:S(2)}) %all-to-all-start.2) | async-done | bytes 12582944 | tf_op jit(solution)/shard_map/all_to_all | solution.py:61
  866.9 14.1 %convolution_bitcast_fusion = f32[16,4,128,768]{2,3,1,0:T(8,128)} fusion(bf16[16,4,128,768]{2,3,1,0:T(8,128)(2,1)} %all-to-all-done.2, s32[16,4,128,128]{3,2,1,0:T(8,128)} %param.10), kind=kOutput, calls=%fused_computation.7 | convolution fusion | flops 1611661312 | bytes 41943040 | tf_op jit(solution)/shard_map/ncab,ncbd->ncad/dot_general | solution.py:62
  881.0 25.1 %copy.38 = f32[8,8,128,768]{3,1,2,0:T(8,128)} copy(f32[8,8,128,768]{2,3,1,0:T(8,128)} %bitcast.30) | data formatting | bytes 50331648
  906.1 14.3 %fusion.4 = f32[16,98304]{1,0:T(8,128)} fusion(f32[64,98304]{1,0:T(8,128)} %bitcast.31, s32[64]{0:T(128)S(1)} %eq.34), kind=kOutput, calls=%fused_computation.21 | convolution fusion | flops 1207960576 | bytes 31457536 | tf_op jit(solution)/shard_map/dot_general | solution.py:66
  920.4 5.2 reshape.72
  (46 shorter events, 21.1 us)
Async XLA Ops:
  7.2 9.0 copy-start
  8.7 25.4 %all-to-all-start = ((s32[16,1,4]{2,1,0:T(1,128)}), s32[16,1,4]{2,1,0:T(1,128)S(1)}, u32[]{:S(2)}, u32[]{:S(2)}) async-start(s32[16,1,4]{2,1,0:T(1,128)} %copy.27), calls=%async_computation | async-start | bytes 16384 | tf_op jit(solution)/shard_map/all_to_all | solution.py:38
  34.1 227.5 %all-to-all-start.1 = ((bf16[16,4,128,768]{2,3,1,0:T(8,128)(2,1)}), bf16[16,4,128,768]{2,3,1,0:T(8,128)(2,1)}, u32[]{:S(2)}, u32[]{:S(2)}) async-start(bf16[16,4,128,768]{2,3,1,0:T(8,128)(2,1)} %convert_bitcast_fusion), calls=%async_computation.1 | async-start | bytes 25165824 | tf_op jit(solution)/shard_map/all_to_all | solution.py:37
  40.8 481.7 %all-gather.6.cloned.1.call-start = ((), (), s32[]{:S(2)}) async-start(), calls=%async_computation.4 | async-start | bytes 56623104 | tf_op jit(solution)/shard_map/all_gather | solution.py:50
  287.3 282.7 %all-gather.4.cloned.1.call-start = ((), (), s32[]{:S(2)}) async-start(), calls=%async_computation.3 | async-start | bytes 3342336 | tf_op jit(solution)/shard_map/all_gather | solution.py:15
  547.6 4.6 copy-start.2
  552.6 29.5 %copy-start.5 = (bf16[2048,768]{1,0:T(8,128)(2,1)}, bf16[2048,768]{1,0:T(8,128)(2,1)S(1)}, u32[]{:S(2)}) copy-start(bf16[2048,768]{1,0:T(8,128)(2,1)S(1)} %multiply_convert_fusion.1) | copy-start | bytes 9437188
  590.2 7.5 copy-start.7
  597.7 7.3 copy-start.4
  639.6 7.4 copy-start.6
  639.6 227.3 %all-to-all-start.2 = ((bf16[16,4,128,768]{2,3,1,0:T(8,128)(2,1)}), bf16[16,4,128,768]{2,3,1,0:T(8,128)(2,1)}, u32[]{:S(2)}, u32[]{:S(2)}) async-start(bf16[16,4,128,768]{2,3,1,0:T(8,128)(2,1)} %broadcast_select_fusion), calls=%async_computation.2 | async-start | bytes 25165824 | tf_op jit(solution)/shard_map/all_to_all | solution.py:61
  920.4 11.8 %copy-start.1 = (bf16[2048,768]{1,0:T(8,128)(2,1)S(1)}, bf16[2048,768]{1,0:T(8,128)(2,1)}, u32[]{:S(2)}) copy-start(bf16[2048,768]{1,0:T(8,128)(2,1)} %param.6) | copy-start | bytes 9437188
  925.6 4.6 copy-start.3
Sparse Core Ops, SparseCore 0:
  287.4 234.9 all-gather.5
  524.6 45.3 all-gather.3
